TPU v7x, 32 devices: a whole 2x2x4 slice. The times are simulated.
32 devices in a mesh: batch: 8 (over z, x), seq: 4 (over y, core).
Axes of the slice: x: 2, y: 2, z: 4, core: 2. Of those that a mesh axis runs over, the one named last changes fastest.
Arguments:
- tokens: bfloat16 [8, 1024, 1024], P('batch', 'seq'), may hold values from -6 to 6
- cotangent: bfloat16 [8, 1024, 1024], P('batch', 'seq'), may hold values from -6 to 6
- image_tokens: bfloat16 [8, 1025, 768], P('batch'), may hold values from -6 to 6
- image_lengths: int32 [8], P('batch'), may hold values from 512 to 1025, as said below
- key_mask: int32 [8, 1025], P('batch'), may hold values 0 or 1
- camera: bfloat16 [8, 1024], P(None, 'batch'), may hold values from -6 to 6
- modulation: bfloat16 [1024, 6144], P('batch'), may hold values from -0.1875 to 0.1875
- q_cross: bfloat16 [1024, 1024], P('batch'), may hold values from -0.1875 to 0.1875
- kv_image: bfloat16 [768, 2048], P('batch'), may hold values from -0.21875 to 0.21875
- out_cross: bfloat16 [1024, 1024], P('batch'), may hold values from -3.5 to 3.5
- qkv_self: bfloat16 [1024, 3072], P('batch'), may hold values from -0.1875 to 0.1875
- out_self: bfloat16 [1024, 1024], P('batch'), may hold values from -6 to 6
- mlp_in: bfloat16 [1024, 4096], P('batch'), may hold values from -0.1875 to 0.1875
- mlp_out: bfloat16 [4096, 1024], P('batch'), may hold values from -0.09375 to 0.09375
Outputs:
- output: bfloat16 [8, 1024, 1024], P('batch', 'seq')
- grad_tokens: float32 [8, 1024, 1024], P('batch', 'seq')
- grad_modulation: float32 [1024, 6144], P('batch')
- grad_q_cross: float32 [1024, 1024], P('batch')
- grad_kv_image: float32 [768, 2048], P('batch')
- grad_out_cross: float32 [1024, 1024], P('batch')
- grad_qkv_self: float32 [1024, 3072], P('batch')
- grad_out_self: float32 [1024, 1024], P('batch')
- grad_mlp_in: float32 [1024, 4096], P('batch')
- grad_mlp_out: float32 [4096, 1024], P('batch')
Inputs may be any that keep to these rules, and one draw needn't show every extreme that they name: `image_lengths`: some object has 1025 valid image tokens and some has 512.
All inputs are finite; a program needn't handle non-finite values. No bound on the sum of `key_mask` on one device may be relied on, other than what follows from the above.
Results may differ from a plain program's by a relative error of at most 0.025.
The roundings to bfloat16 on the way count: a program that leaves them out, or rounds other values in their place, can miss the bound.
Values may be sent and summed in bfloat16 or wider, within the bound.
A program may use at most 256 MiB of HBM per device.

v0:
```python
import jax
import jax.numpy as jnp
from jax import lax
from jax.sharding import PartitionSpec as P

HEADS = 16
HEAD_DIM = 64
epsilon = 1e-06
group_heads = 4
highest = lax.Precision.HIGHEST


def modulated_norm(values, shift, scale):
    center = values - jnp.mean(values, axis=-1, keepdims=True)
    normed = center * lax.rsqrt(jnp.mean(center * center, axis=-1, keepdims=True) + epsilon)
    return normed * (1.0 + scale) + shift


def product(left, right):
    return jnp.dot(left, right, preferred_element_type=jnp.float32)


def contract_rows(left, right):
    return lax.dot_general(
        left, right, (((0,), (0,)), ((), ())), preferred_element_type=jnp.float32
    )


def times_transposed(left, right):
    return lax.dot_general(
        left, right, (((1,), (1,)), ((), ())), preferred_element_type=jnp.float32
    )


def split_heads(values):
    rows = values.shape[0]
    grouped = values.reshape(rows, HEADS // group_heads, group_heads, HEAD_DIM)
    return grouped.transpose(1, 2, 0, 3)


def join_heads(values):
    groups, inner, rows, depth = values.shape
    return values.transpose(2, 0, 1, 3).reshape(rows, groups * inner * depth)


def scores_of(query_group, key_group, valid):
    scores = jnp.einsum(
        "hqd,hkd->hqk", query_group, key_group, preferred_element_type=jnp.float32
    ) * HEAD_DIM ** (-0.5)
    return jnp.where(valid[None, None, :], scores, -1000000000.0)


def attend_forward(query, key_rows, value_rows, valid):

    def one_group(pieces):
        query_group, key_group, value_group = pieces
        scores = scores_of(query_group, key_group, valid)
        top = jnp.max(scores, axis=-1, keepdims=True)
        expo = jnp.exp(scores - top)
        total = jnp.sum(expo, axis=-1, keepdims=True)
        probs = (expo / total).astype(jnp.bfloat16)
        result = jnp.einsum("hqk,hkd->hqd", probs, value_group, preferred_element_type=jnp.float32)
        return (result, top, total)

    results, tops, totals = lax.map(
        one_group, (split_heads(query), split_heads(key_rows), split_heads(value_rows))
    )
    return (join_heads(results), (tops, totals))


def attend_backward(query, key_rows, value_rows, valid, stats, grad_output):
    tops, totals = stats

    def one_group(pieces):
        query_group, key_group, value_group, top, total, grad_group = pieces
        scores = scores_of(query_group, key_group, valid)
        probs = jnp.exp(scores - top) / total
        grad_probs = jnp.einsum(
            "hqd,hkd->hqk", grad_group, value_group, preferred_element_type=jnp.float32
        )
        inner = jnp.sum(probs * grad_probs, axis=-1, keepdims=True)
        grad_scores = (probs * (grad_probs - inner)).astype(jnp.bfloat16)
        factor = HEAD_DIM ** (-0.5)
        grad_query = (
            jnp.einsum("hqk,hkd->hqd", grad_scores, key_group, preferred_element_type=jnp.float32)
            * factor
        )
        grad_keys = (
            jnp.einsum("hqk,hqd->hkd", grad_scores, query_group, preferred_element_type=jnp.float32)
            * factor
        )
        grad_values = jnp.einsum(
            "hqk,hqd->hkd",
            probs.astype(jnp.bfloat16),
            grad_group,
            preferred_element_type=jnp.float32,
        )
        return (grad_query, inner, grad_keys, grad_values)

    results = lax.map(
        one_group,
        (
            split_heads(query),
            split_heads(key_rows),
            split_heads(value_rows),
            tops,
            totals,
            split_heads(grad_output),
        ),
    )
    return (join_heads(results[0]), results[1], join_heads(results[2]), join_heads(results[3]))


def local(
    tokens,
    cotangent,
    image_tokens,
    image_lengths,
    key_mask,
    camera,
    modulation,
    q_cross,
    kv_image,
    out_cross,
    qkv_self,
    out_self,
    mlp_in,
    mlp_out,
):
    q_full, kv_full, out_cross_full, qkv_full, out_self_full, mlp_in_full, mlp_out_full = (
        lax.all_gather(q_cross, "batch", axis=0, tiled=True),
        lax.all_gather(kv_image, "batch", axis=0, tiled=True),
        lax.all_gather(out_cross, "batch", axis=0, tiled=True),
        lax.all_gather(qkv_self, "batch", axis=0, tiled=True),
        lax.all_gather(out_self, "batch", axis=0, tiled=True),
        lax.all_gather(mlp_in, "batch", axis=0, tiled=True),
        lax.all_gather(mlp_out, "batch", axis=0, tiled=True),
    )
    camera_gate = jax.nn.silu(camera.astype(jnp.float32)).astype(jnp.bfloat16)
    modulation_all = lax.psum(product(camera_gate, modulation), "batch")
    object_index = lax.axis_index("batch")
    width = tokens.shape[2]
    shifts = lax.dynamic_index_in_dim(modulation_all, object_index, 0, keepdims=False).reshape(
        6, width
    )
    stream = tokens[0].astype(jnp.float32)
    image_rows = image_tokens[0]
    positions = jnp.arange(image_rows.shape[0], dtype=jnp.int32)
    valid = (positions < image_lengths[0]) & ((key_mask[0] == 1) | (positions == 0))
    everywhere = jnp.ones((lax.axis_size("seq") * stream.shape[0],), dtype=jnp.bool_)
    normed_cross, cross_pullback = jax.vjp(modulated_norm, stream, shifts[0], shifts[1])
    normed_cross = normed_cross.astype(jnp.bfloat16)
    query_cross = product(normed_cross, q_full).astype(jnp.bfloat16)
    image_kv = product(image_rows, kv_full)
    image_keys = image_kv[:, :width].astype(jnp.bfloat16)
    image_values = image_kv[:, width:].astype(jnp.bfloat16)
    attended_cross, cross_stats = attend_forward(query_cross, image_keys, image_values, valid)
    attended_cross = attended_cross.astype(jnp.bfloat16)
    after_cross = stream + product(attended_cross, out_cross_full)
    normed_self, self_pullback = jax.vjp(modulated_norm, after_cross, shifts[2], shifts[3])
    normed_self = normed_self.astype(jnp.bfloat16)
    packed = product(normed_self, qkv_full).astype(jnp.bfloat16)
    query_self = packed[:, :width]
    key_local = packed[:, width : 2 * width]
    value_local = packed[:, 2 * width :]
    key_whole, value_whole = (
        lax.all_gather(key_local, "seq", axis=0, tiled=True),
        lax.all_gather(value_local, "seq", axis=0, tiled=True),
    )
    attended_self, self_stats = attend_forward(query_self, key_whole, value_whole, everywhere)
    attended_self = attended_self.astype(jnp.bfloat16)
    after_self = after_cross + product(attended_self, out_self_full)
    normed_mlp, mlp_pullback = jax.vjp(modulated_norm, after_self, shifts[4], shifts[5])
    normed_mlp = normed_mlp.astype(jnp.bfloat16)
    up_rows = product(normed_mlp, mlp_in_full)
    hidden, gelu_pullback = jax.vjp(jax.nn.gelu, up_rows)
    hidden = hidden.astype(jnp.bfloat16)
    output = after_self + product(hidden, mlp_out_full)
    grad_stream = cotangent[0].astype(jnp.float32)
    grad_branch = grad_stream.astype(jnp.bfloat16)
    grad_mlp_out = contract_rows(hidden, grad_branch)
    (grad_up,) = gelu_pullback(times_transposed(grad_branch, mlp_out_full))
    grad_up = grad_up.astype(jnp.bfloat16)
    grad_mlp_in = contract_rows(normed_mlp, grad_up)
    grad_from, shift_mlp, scale_mlp = mlp_pullback(times_transposed(grad_up, mlp_in_full))
    grad_stream = grad_stream + grad_from
    grad_branch = grad_stream.astype(jnp.bfloat16)
    grad_out_self = contract_rows(attended_self, grad_branch)
    grad_attended = times_transposed(grad_branch, out_self_full).astype(jnp.bfloat16)
    grad_query, inner_local, key_terms, value_terms = attend_backward(
        query_self, key_whole, value_whole, everywhere, self_stats, grad_attended
    )
    grad_key, grad_value = (
        lax.psum_scatter(key_terms, "seq", scatter_dimension=0, tiled=True),
        lax.psum_scatter(value_terms, "seq", scatter_dimension=0, tiled=True),
    )
    grad_packed = jnp.concatenate([grad_query, grad_key, grad_value], axis=1).astype(jnp.bfloat16)
    grad_qkv_self = contract_rows(normed_self, grad_packed)
    grad_from, shift_self, scale_self = self_pullback(times_transposed(grad_packed, qkv_full))
    grad_stream = grad_stream + grad_from
    grad_branch = grad_stream.astype(jnp.bfloat16)
    grad_out_cross = contract_rows(attended_cross, grad_branch)
    grad_attended = times_transposed(grad_branch, out_cross_full).astype(jnp.bfloat16)
    grad_query, inner_cross, key_terms, value_terms = attend_backward(
        query_cross, image_keys, image_values, valid, cross_stats, grad_attended
    )
    image_float = image_rows.astype(jnp.float32)
    image_key_grad, image_value_grad = (
        lax.psum_scatter(
            key_terms.astype(jnp.bfloat16), "seq", scatter_dimension=1, tiled=True
        ).astype(jnp.float32),
        lax.psum_scatter(
            value_terms.astype(jnp.bfloat16), "seq", scatter_dimension=1, tiled=True
        ).astype(jnp.float32),
    )
    block_width = image_key_grad.shape[1]
    column_start = lax.axis_index("seq") * block_width
    image_grads = jnp.concatenate([image_key_grad, image_value_grad], axis=1)
    kv_block = lax.dot_general(
        image_float,
        image_grads,
        (((0,), (0,)), ((), ())),
        precision=highest,
        preferred_element_type=jnp.float32,
    )
    grad_kv_image = jnp.zeros((image_rows.shape[1], 2 * width), jnp.float32)
    grad_kv_image = lax.dynamic_update_slice(
        grad_kv_image, kv_block[:, :block_width], (jnp.int32(0), column_start)
    )
    grad_kv_image = lax.dynamic_update_slice(
        grad_kv_image, kv_block[:, block_width:], (jnp.int32(0), column_start + width)
    )
    grad_query = grad_query.astype(jnp.bfloat16)
    grad_q_cross = contract_rows(normed_cross, grad_query)
    grad_from, shift_cross, scale_cross = cross_pullback(times_transposed(grad_query, q_full))
    grad_input = grad_stream + grad_from
    grad_row = jnp.concatenate(
        [shift_cross, scale_cross, shift_self, scale_self, shift_mlp, scale_mlp]
    )
    grad_table = lax.dynamic_update_slice(
        jnp.zeros(modulation_all.shape, jnp.float32),
        grad_row[None, :],
        (object_index, jnp.int32(0)),
    )
    grad_table = lax.psum(grad_table, ("batch", "seq"))
    grad_modulation = lax.dot_general(
        camera_gate.astype(jnp.float32),
        grad_table,
        (((0,), (0,)), ((), ())),
        precision=highest,
        preferred_element_type=jnp.float32,
    )
    terms = (
        grad_q_cross,
        grad_kv_image,
        grad_out_cross,
        grad_qkv_self,
        grad_out_self,
        grad_mlp_in,
        grad_mlp_out,
    )
    shares = (
        lax.psum_scatter(
            terms[0].astype(jnp.bfloat16), "batch", scatter_dimension=0, tiled=True
        ).astype(jnp.float32),
        lax.psum_scatter(
            terms[1].astype(jnp.bfloat16), "batch", scatter_dimension=0, tiled=True
        ).astype(jnp.float32),
        lax.psum_scatter(
            terms[2].astype(jnp.bfloat16), "batch", scatter_dimension=0, tiled=True
        ).astype(jnp.float32),
        lax.psum_scatter(
            terms[3].astype(jnp.bfloat16), "batch", scatter_dimension=0, tiled=True
        ).astype(jnp.float32),
        lax.psum_scatter(
            terms[4].astype(jnp.bfloat16), "batch", scatter_dimension=0, tiled=True
        ).astype(jnp.float32),
        lax.psum_scatter(
            terms[5].astype(jnp.bfloat16), "batch", scatter_dimension=0, tiled=True
        ).astype(jnp.float32),
        lax.psum_scatter(
            terms[6].astype(jnp.bfloat16), "batch", scatter_dimension=0, tiled=True
        ).astype(jnp.float32),
    )
    totals = (
        lax.psum(shares[0].astype(jnp.bfloat16), "seq").astype(jnp.float32),
        lax.psum(shares[1].astype(jnp.bfloat16), "seq").astype(jnp.float32),
        lax.psum(shares[2].astype(jnp.bfloat16), "seq").astype(jnp.float32),
        lax.psum(shares[3].astype(jnp.bfloat16), "seq").astype(jnp.float32),
        lax.psum(shares[4].astype(jnp.bfloat16), "seq").astype(jnp.float32),
        lax.psum(shares[5].astype(jnp.bfloat16), "seq").astype(jnp.float32),
        lax.psum(shares[6].astype(jnp.bfloat16), "seq").astype(jnp.float32),
    )
    return (
        output.astype(jnp.bfloat16)[None],
        grad_input[None],
        grad_modulation,
        totals[0],
        totals[1],
        totals[2],
        totals[3],
        totals[4],
        totals[5],
        totals[6],
    )


def solution(mesh):
    return jax.shard_map(
        local,
        mesh=mesh,
        in_specs=(
            P("batch", "seq", None),
            P("batch", "seq", None),
            P("batch", None, None),
            P("batch"),
            P("batch", None),
            P(None, "batch"),
            P("batch", None),
            P("batch", None),
            P("batch", None),
            P("batch", None),
            P("batch", None),
            P("batch", None),
            P("batch", None),
            P("batch", None),
        ),
        out_specs=(
            P("batch", "seq", None),
            P("batch", "seq", None),
            P("batch", None),
            P("batch", None),
            P("batch", None),
            P("batch", None),
            P("batch", None),
            P("batch", None),
            P("batch", None),
            P("batch", None),
        ),
        check_vma=False,
    )
```

profile of v0, /device:TPU:0, one launch (start us, length us, event | category | flops | bytes accessed | tf_op | source)
XLA Modules:
  0.0 1926.2 jit_solution(18248695921334428257)
XLA Ops:
  15.5 69.2 %all-reduce.5.cloned.1.call-done = f32[8,6144]{1,0:T(8,128)} async-done(((f32[8,6144]{1,0:T(8,128)}), f32[8,6144]{1,0:T(8,128)}) %all-reduce.5.cloned.1.call-update) | async-done | bytes 196624 | tf_op jit(solution)/shard_map/psum | solution.py:140
  85.7 49.7 %all-gather.10.cloned.1.call-done = bf16[1024,1024]{1,0:T(8,128)(2,1)} async-done(((bf16[128,1024]{1,0:T(8,128)(2,1)}), bf16[1024,1024]{1,0:T(8,128)(2,1)}) %all-gather.10.cloned.1.call-update) | async-done | bytes 2097168 | tf_op jit(solution)/shard_map/all_gather | solution.py:131
  138.0 58.8 %all-gather.12.cloned.1.call-done = bf16[768,2048]{1,0:T(8,128)(2,1)} async-done(((bf16[96,2048]{1,0:T(8,128)(2,1)}), bf16[768,2048]{1,0:T(8,128)(2,1)}) %all-gather.12.cloned.1.call-update) | async-done | bytes 3145744 | tf_op jit(solution)/shard_map/all_gather | solution.py:132
  196.8 5.6 convolution_convert_fusion.2
  205.0 4.0 copy.35
  209.0 4.1 copy.36
  213.2 18.4 while.56
  231.7 15.3 all-gather.14.cloned.1.call-done
  247.0 2.6 fusion.167
  249.9 96.9 %all-gather.16.cloned.1.call-done = bf16[1024,3072]{1,0:T(8,128)(2,1)} async-done(((bf16[128,3072]{1,0:T(8,128)(2,1)}), bf16[1024,3072]{1,0:T(8,128)(2,1)}) %all-gather.16.cloned.1.call-update) | async-done | bytes 6291472 | tf_op jit(solution)/shard_map/all_gather | solution.py:134
  346.8 4.7 convolution_convert_fusion.4
  357.0 16.6 all-gather.18.cloned.1.call-done
  373.6 3.9 copy.38
  377.6 20.9 %all-gather.20.cloned.1.call-done = bf16[1024,1024]{1,0:T(8,128)(2,1)} async-done(((bf16[256,1024]{1,0:T(8,128)(2,1)}), bf16[1024,1024]{1,0:T(8,128)(2,1)}) %all-gather.20.cloned.1.call-update) | async-done | bytes 2097168 | tf_op jit(solution)/shard_map/all_gather | solution.py:168
  398.5 3.9 copy.39
  403.3 23.0 %while.57 = (s32[]{:T(128)}, bf16[4,4,256,64]{2,3,1,0:T(8,128)(2,1)}, f32[4,4,256,1]{2,1,3,0:T(4,128)S(1)}, f32[4,4,256,1]{2,1,3,0:T(4,128)S(1)}, bf16[4,4,256,6...) while((s32[]{:T(128)}, ...), condition=%wide.region_12.13_spmd, body=%wide.region_9.12_spmd.sunk | while | flops 277870592 | bytes 18258072 | solution.py:65
  426.2 24.1 %all-gather.22.cloned.1.call-done = bf16[1024,1024]{1,0:T(8,128)(2,1)} async-done(((bf16[128,1024]{1,0:T(8,128)(2,1)}), bf16[1024,1024]{1,0:T(8,128)(2,1)}) %all-gather.22.cloned.1.call-update) | async-done | bytes 2097168 | tf_op jit(solution)/shard_map/all_gather | solution.py:135
  450.4 2.6 fusion.168
  454.2 122.0 %all-gather.24.cloned.1.call-done = bf16[1024,4096]{1,0:T(8,128)(2,1)} async-done(((bf16[128,4096]{1,0:T(8,128)(2,1)}), bf16[1024,4096]{1,0:T(8,128)(2,1)}) %all-gather.24.cloned.1.call-update) | async-done | bytes 8388624 | tf_op jit(solution)/shard_map/all_gather | solution.py:136
  576.2 8.1 fusion.160
  584.3 117.2 %all-gather.26.cloned.1.call-done = bf16[4096,1024]{1,0:T(8,128)(2,1)} async-done(((bf16[512,1024]{1,0:T(8,128)(2,1)}), bf16[4096,1024]{1,0:T(8,128)(2,1)}) %all-gather.26.cloned.1.call-update) | async-done | bytes 8388624 | tf_op jit(solution)/shard_map/all_gather | solution.py:137
  701.5 9.3 fusion.95
  710.8 3.2 multiply_reduce_fusion.3
  720.9 39.8 %while.58 = (s32[]{:T(128)}, bf16[4,4,256,64]{2,3,1,0:T(8,128)(2,1)}, f32[4,4,1024,64]{2,3,1,0:T(8,128)}, f32[4,4,1024,64]{2,3,1,0:T(8,128)}, bf16[4,4,256,64]{2...) while((s32[]{:T(128)}, ...), condition=%wide.region_19.20_spmd, body=%wide.region_17.19_spmd.sunk | while | flops 680852480 | bytes 48534732 | solution.py:100
  761.4 42.2 %reduce-scatter.14.cloned.1.call-done = f32[256,1024]{0,1:T(8,128)} async-done(((f32[1024,1024]{0,1:T(8,128)}), f32[256,1024]{0,1:T(8,128)}) %reduce-scatter.14.cloned.1.call-update) | async-done | bytes 1048592 | tf_op jit(solution)/shard_map/reduce_scatter | solution.py:195
  804.9 45.6 %reduce-scatter.12.cloned.1.call-done = f32[256,1024]{0,1:T(8,128)} async-done(((f32[1024,1024]{0,1:T(8,128)}), f32[256,1024]{0,1:T(8,128)}) %reduce-scatter.12.cloned.1.call-update) | async-done | bytes 1048592 | tf_op jit(solution)/shard_map/reduce_scatter | solution.py:194
  851.8 5.9 multiply_reduce_fusion.4
  863.9 40.3 %while.59 = (s32[]{:T(128)}, bf16[4,4,256,64]{2,3,1,0:T(8,128)(2,1)}, bf16[4,4,1025,64]{2,3,1,0:T(8,128)(2,1)}, bf16[4,4,1025,64]{2,3,1,0:T(8,128)(2,1)}, pred[1...) while((s32[]{:T(128)}, ...), condition=%wide.region_26.27_spmd, body=%wide.region_24.26_spmd.sunk | while | flops 682566912 | bytes 82707776 | solution.py:100
  904.9 3.3 convolution_convert_fusion.5
  908.5 3.3 convolution_convert_fusion.7
  911.8 3.7 convolution_convert_fusion.6
  915.6 7.7 convolution_convert_fusion.1
  923.4 8.6 convolution_convert_fusion
  932.0 5.4 reduce-scatter.20.cloned.1.call-done
  937.4 35.5 %reduce-scatter.18.cloned.1.call-done = bf16[1025,256]{0,1:T(8,128)(2,1)} async-done(((bf16[1025,1024]{0,1:T(8,128)(2,1)}), bf16[1025,256]{0,1:T(8,128)(2,1)}) %reduce-scatter.18.cloned.1.call-update) | async-done | bytes 524816 | tf_op jit(solution)/shard_map/reduce_scatter | solution.py:209
  982.9 6.3 convolution_convert_fusion.3
  989.9 2.7 fusion.118
  995.6 48.8 %reduce-scatter.28.cloned.1.call-done = bf16[128,1024]{1,0:T(8,128)(2,1)} async-done(((bf16[1024,1024]{1,0:T(8,128)(2,1)}), bf16[128,1024]{1,0:T(8,128)(2,1)}) %reduce-scatter.28.cloned.1.call-update) | async-done | bytes 262160 | tf_op jit(solution)/shard_map/reduce_scatter | solution.py:275
  1044.4 71.2 %reduce-scatter.16.cloned.1.call-done = bf16[128,1024]{1,0:T(8,128)(2,1)} async-done(((bf16[1024,1024]{1,0:T(8,128)(2,1)}), bf16[128,1024]{1,0:T(8,128)(2,1)}) %reduce-scatter.16.cloned.1.call-update) | async-done | bytes 262160 | tf_op jit(solution)/shard_map/reduce_scatter | solution.py:263
  1115.6 71.3 %reduce-scatter.24.cloned.1.call-done = bf16[128,1024]{1,0:T(8,128)(2,1)} async-done(((bf16[1024,1024]{1,0:T(8,128)(2,1)}), bf16[128,1024]{1,0:T(8,128)(2,1)}) %reduce-scatter.24.cloned.1.call-update) | async-done | bytes 262160 | tf_op jit(solution)/shard_map/reduce_scatter | solution.py:269
  1186.9 152.0 %reduce-scatter.30.cloned.1.call-done = bf16[128,4096]{1,0:T(8,128)(2,1)} async-done(((bf16[1024,4096]{1,0:T(8,128)(2,1)}), bf16[128,4096]{1,0:T(8,128)(2,1)}) %reduce-scatter.30.cloned.1.call-update) | async-done | bytes 1048592 | tf_op jit(solution)/shard_map/reduce_scatter | solution.py:278
  1338.9 151.7 %reduce-scatter.32.cloned.1.call-done = bf16[512,1024]{1,0:T(8,128)(2,1)} async-done(((bf16[4096,1024]{1,0:T(8,128)(2,1)}), bf16[512,1024]{1,0:T(8,128)(2,1)}) %reduce-scatter.32.cloned.1.call-update) | async-done | bytes 1048592 | tf_op jit(solution)/shard_map/reduce_scatter | solution.py:281
  1490.6 77.8 %reduce-scatter.22.cloned.1.call-done = bf16[96,2048]{1,0:T(8,128)(2,1)} async-done(((bf16[768,2048]{1,0:T(8,128)(2,1)}), bf16[96,2048]{1,0:T(8,128)(2,1)}) %reduce-scatter.22.cloned.1.call-update) | async-done | bytes 393232 | tf_op jit(solution)/shard_map/reduce_scatter | solution.py:266
  1568.4 121.2 %reduce-scatter.26.cloned.1.call-done = bf16[128,3072]{1,0:T(8,128)(2,1)} async-done(((bf16[1024,3072]{1,0:T(8,128)(2,1)}), bf16[128,3072]{1,0:T(8,128)(2,1)}) %reduce-scatter.26.cloned.1.call-update) | async-done | bytes 786448 | tf_op jit(solution)/shard_map/reduce_scatter | solution.py:272
  1689.7 8.3 fusion.108
  1699.4 119.4 %all-reduce.7.cloned.1.call-done = f32[8,6144]{1,0:T(8,128)} async-done(((f32[8,6144]{1,0:T(8,128)}), f32[8,6144]{1,0:T(8,128)}) %all-reduce.7.cloned.1.call-update) | async-done | bytes 196624 | tf_op jit(solution)/shard_map/psum | solution.py:245
  1818.8 4.0 fusion.155
  1822.9 84.5 %all-reduce.9.cloned.1.call-done = (bf16[128,1024]{1,0:T(8,128)(2,1)}, bf16[96,2048]{1,0:T(8,128)(2,1)}, bf16[128,1024]{1,0:T(8,128)(2,1)}, bf16[128,3072]{1,0:T...) async-done(((bf16[128,1024]{1,0:T(8,128)(2,1)}, bf16[96,2048]{1,0:T(8,128)(2,1)}, bf16[128,1024]{1,0:T(8,128)(2,1)}, ...) | async-done | bytes 4063248 | tf_op jit(solution)/shard_map/psum | solution.py:286
  (419 shorter events, 185.9 us)
Async XLA Ops:
  7.2 189.7 %copy-start = (bf16[1,1025,768]{2,1,0:T(8,128)(2,1)S(1)}, bf16[1,1025,768]{2,1,0:T(8,128)(2,1)}, u32[]{:S(2)}) copy-start(bf16[1,1025,768]{2,1,0:T(8,128)(2,1)} %param.24) | copy-start | bytes 4723204
  7.2 77.5 %all-reduce.5.cloned.1.call-start = ((), (), s32[]{:S(2)}) async-start(), calls=%async_computation.11 | async-start | bytes 393216 | tf_op jit(solution)/shard_map/psum | solution.py:140
  9.8 125.6 %all-gather.10.cloned.1.call-start = ((), (), s32[]{:S(2)}) async-start(), calls=%async_computation.12 | async-start | bytes 2359296 | tf_op jit(solution)/shard_map/all_gather | solution.py:131
  10.6 186.2 %all-gather.12.cloned.1.call-start = ((), (), s32[]{:S(2)}) async-start(), calls=%async_computation.13 | async-start | bytes 3538944 | tf_op jit(solution)/shard_map/all_gather | solution.py:132
  11.3 235.6 %all-gather.14.cloned.1.call-start = ((), (), s32[]{:S(2)}) async-start(), calls=%async_computation.14 | async-start | bytes 2359296 | tf_op jit(solution)/shard_map/all_gather | solution.py:133
  11.9 334.9 %all-gather.16.cloned.1.call-start = ((), (), s32[]{:S(2)}) async-start(), calls=%async_computation.15 | async-start | bytes 7077888 | tf_op jit(solution)/shard_map/all_gather | solution.py:134
  12.5 361.1 %all-gather.18.cloned.1.call-start = ((), (), s32[]{:S(2)}) async-start(), calls=%async_computation.16 | async-start | bytes 2621440 | tf_op jit(solution)/shard_map/all_gather | solution.py:167
  15.1 187.3 %copy-start.49 = (f32[256]{0:T(256)}, f32[256]{0:T(256)S(1)}, u32[]{:S(2)}) copy-start(f32[256]{0:T(256)S(1)} %broadcast_multiply_fusion.2) | copy-start | bytes 3076
  15.4 120.0 %copy-start.63 = (f32[256]{0:T(256)}, f32[256]{0:T(256)S(1)}, u32[]{:S(2)}) copy-start(f32[256]{0:T(256)S(1)} %fusion.117) | copy-start | bytes 3076
  15.4 187.0 %copy-start.55 = (f32[256]{0:T(256)}, f32[256]{0:T(256)S(1)}, u32[]{:S(2)}) copy-start(f32[256]{0:T(256)S(1)} %fusion.149) | copy-start | bytes 3076
  85.7 116.8 %copy-start.46 = (f32[1,1024]{1,0:T(1,128)}, f32[1,1024]{1,0:T(1,128)S(1)}, u32[]{:S(2)}) copy-start(f32[1,1024]{1,0:T(1,128)S(1)} %get-tuple-element.337) | copy-start | bytes 12292
  85.7 116.8 %copy-start.61 = (f32[1,1024]{1,0:T(1,128)}, f32[1,1024]{1,0:T(1,128)S(1)}, u32[]{:S(2)}) copy-start(f32[1,1024]{1,0:T(1,128)S(1)} %get-tuple-element.336) | copy-start | bytes 12292
  85.7 261.1 %copy-start.41 = (f32[1,1024]{1,0:T(1,128)}, f32[1,1024]{1,0:T(1,128)S(1)}, u32[]{:S(2)}) copy-start(f32[1,1024]{1,0:T(1,128)S(1)} %get-tuple-element.334) | copy-start | bytes 12292
  85.7 490.5 %copy-start.42 = (f32[1,1024]{1,0:T(1,128)}, f32[1,1024]{1,0:T(1,128)S(1)}, u32[]{:S(2)}) copy-start(f32[1,1024]{1,0:T(1,128)S(1)} %get-tuple-element.338) | copy-start | bytes 12292
  85.7 628.4 %copy-start.39 = (f32[1,1024]{1,0:T(1,128)}, f32[1,1024]{1,0:T(1,128)S(1)}, u32[]{:S(2)}) copy-start(f32[1,1024]{1,0:T(1,128)S(1)} %get-tuple-element.333) | copy-start | bytes 12292
  231.7 15.3 copy-start.13
  231.7 15.3 copy-start.15
  231.7 119.8 %copy-start.44 = (pred[1025]{0:T(1024)(128)(4,1)}, pred[1025]{0:T(1024)(128)(4,1)S(1)}, u32[]{:S(2)}) copy-start(pred[1025]{0:T(1024)(128)(4,1)S(1)} %get-tuple-element.833) | copy-start | bytes 3079
  249.6 608.1 %copy-start.52 = (f32[256]{0:T(256)}, f32[256]{0:T(256)S(1)}, u32[]{:S(2)}) copy-start(f32[256]{0:T(256)S(1)} %broadcast_multiply_fusion.1) | copy-start | bytes 3076
  249.9 607.8 %copy-start.58 = (f32[256]{0:T(256)}, f32[256]{0:T(256)S(1)}, u32[]{:S(2)}) copy-start(f32[256]{0:T(256)S(1)} %fusion.150) | copy-start | bytes 3076
  352.7 45.8 %all-gather.20.cloned.1.call-start = ((), (), s32[]{:S(2)}) async-start(), calls=%async_computation.17 | async-start | bytes 2621440 | tf_op jit(solution)/shard_map/all_gather | solution.py:168
  353.4 96.9 %all-gather.22.cloned.1.call-start = ((), (), s32[]{:S(2)}) async-start(), calls=%async_computation.18 | async-start | bytes 2359296 | tf_op jit(solution)/shard_map/all_gather | solution.py:135
  354.2 222.0 %all-gather.24.cloned.1.call-start = ((), (), s32[]{:S(2)}) async-start(), calls=%async_computation.19 | async-start | bytes 9437184 | tf_op jit(solution)/shard_map/all_gather | solution.py:136
  354.9 346.6 %all-gather.26.cloned.1.call-start = ((), (), s32[]{:S(2)}) async-start(), calls=%async_computation.20 | async-start | bytes 9437184 | tf_op jit(solution)/shard_map/all_gather | solution.py:137
  355.5 448.1 %reduce-scatter.14.cloned.1.call-start = ((), (), s32[]{:S(2)}) async-start(), calls=%async_computation.22 | async-start | bytes 5242880 | tf_op jit(solution)/shard_map/reduce_scatter | solution.py:195
  453.0 261.1 %copy-start.53 = (f32[256]{0:T(256)}, f32[256]{0:T(256)S(1)}, u32[]{:S(2)}) copy-start(f32[256]{0:T(256)S(1)} %broadcast_multiply_fusion) | copy-start | bytes 3076
  454.2 259.9 %copy-start.59 = (f32[256]{0:T(256)}, f32[256]{0:T(256)S(1)}, u32[]{:S(2)}) copy-start(f32[256]{0:T(256)S(1)} %fusion.151) | copy-start | bytes 3076
  701.5 9.3 copy-start.4
  701.5 9.3 copy-start.70
  760.8 89.7 %reduce-scatter.12.cloned.1.call-start = ((), (), s32[]{:S(2)}) async-start(), calls=%async_computation.21 | async-start | bytes 5242880 | tf_op jit(solution)/shard_map/reduce_scatter | solution.py:194
  761.3 176.1 %reduce-scatter.20.cloned.1.call-start = ((), (), s32[]{:S(2)}) async-start(), calls=%async_computation.26 | async-start | bytes 2949120 | tf_op jit(solution)/shard_map/reduce_scatter | solution.py:212
  804.9 52.8 %copy-start.25 = (bf16[256,1024]{0,1:T(8,128)(2,1)}, bf16[256,1024]{0,1:T(8,128)(2,1)S(1)}, u32[]{:S(2)}) copy-start(bf16[256,1024]{0,1:T(8,128)(2,1)S(1)} %convert.19) | copy-start | bytes 1572868
  904.3 68.7 %reduce-scatter.18.cloned.1.call-start = ((), (), s32[]{:S(2)}) async-start(), calls=%async_computation.25 | async-start | bytes 2949120 | tf_op jit(solution)/shard_map/reduce_scatter | solution.py:209
  904.9 139.5 %reduce-scatter.28.cloned.1.call-start = ((), (), s32[]{:S(2)}) async-start(), calls=%async_computation.30 | async-start | bytes 2359296 | tf_op jit(solution)/shard_map/reduce_scatter | solution.py:275
  908.2 207.4 %reduce-scatter.16.cloned.1.call-start = ((), (), s32[]{:S(2)}) async-start(), calls=%async_computation.24 | async-start | bytes 2359296 | tf_op jit(solution)/shard_map/reduce_scatter | solution.py:263
  911.8 275.1 %reduce-scatter.24.cloned.1.call-start = ((), (), s32[]{:S(2)}) async-start(), calls=%async_computation.28 | async-start | bytes 2359296 | tf_op jit(solution)/shard_map/reduce_scatter | solution.py:269
  915.5 423.4 %reduce-scatter.30.cloned.1.call-start = ((), (), s32[]{:S(2)}) async-start(), calls=%async_computation.31 | async-start | bytes 9437184 | tf_op jit(solution)/shard_map/reduce_scatter | solution.py:278
  923.3 567.3 %reduce-scatter.32.cloned.1.call-start = ((), (), s32[]{:S(2)}) async-start(), calls=%async_computation.32 | async-start | bytes 9437184 | tf_op jit(solution)/shard_map/reduce_scatter | solution.py:281
  932.0 636.4 %reduce-scatter.22.cloned.1.call-start = ((), (), s32[]{:S(2)}) async-start(), calls=%async_computation.27 | async-start | bytes 3538944 | tf_op jit(solution)/shard_map/reduce_scatter | solution.py:266
  982.9 706.8 %reduce-scatter.26.cloned.1.call-start = ((), (), s32[]{:S(2)}) async-start(), calls=%async_computation.29 | async-start | bytes 7077888 | tf_op jit(solution)/shard_map/reduce_scatter | solution.py:272
  989.3 700.4 %copy-start.5 = (f32[256,1024]{1,0:T(8,128)S(1)}, f32[256,1024]{1,0:T(8,128)}, u32[]{:S(2)}) copy-start(f32[256,1024]{1,0:T(8,128)} %copy-done.3) | copy-start | bytes 3145732
  989.3 829.5 %all-reduce.7.cloned.1.call-start = ((), (), s32[]{:S(2)}) async-start(), calls=%async_computation.23 | async-start | bytes 393216 | tf_op jit(solution)/shard_map/psum | solution.py:245
  995.5 911.8 %all-reduce.9.cloned.1.call-start = ((), (), s32[]{:S(2)}) async-start(), calls=%async_computation.33 | async-start | bytes 8126464 | tf_op jit(solution)/shard_map/psum | solution.py:286
  1689.7 8.4 copy-start.9
  1689.7 8.4 copy-start.19
  1689.7 129.1 %copy-start.65 = (bf16[8,128]{1,0:T(8,128)(2,1)S(1)}, bf16[8,128]{1,0:T(8,128)(2,1)}, u32[]{:S(2)}) copy-start(bf16[8,128]{1,0:T(8,128)(2,1)} %param.27) | copy-start | bytes 6148
  1907.4 9.0 copy-start.36
  1909.3 8.6 copy-start.35
  (82 other events, 227.3 us)
Sparse Core Ops, SparseCore 0:
  11.9 72.7 all-reduce.4
  87.1 48.3 all-gather.9
  137.9 58.9 all-gather.11
  199.0 47.9 all-gather.13
  249.2 97.5 all-gather.15
  352.8 20.7 all-gather.17
  375.8 22.5 all-gather.19
  400.8 49.5 all-gather.21
  452.7 123.4 all-gather.23
  578.4 123.1 all-gather.25
  760.9 42.6 reduce-scatter.13
  806.0 44.4 reduce-scatter.11
  904.3 33.0 reduce-scatter.19
  939.8 33.0 reduce-scatter.17
  976.7 67.6 reduce-scatter.27
  1048.8 66.7 reduce-scatter.15
  1120.0 66.8 reduce-scatter.23
  1190.8 148.0 reduce-scatter.29
  1342.5 147.9 reduce-scatter.31
  1495.0 73.3 reduce-scatter.21
  1572.4 117.1 reduce-scatter.25
  1696.7 122.1 all-reduce.6
  1822.0 85.3 all-reduce.8
where the time goes:
time: 1940 us; the launch traced here: 1930 us
  waiting for transfers between devices  1620 us (84%)
  matrix products  195 us (10%)
  local copies, waits for them, and re-layouts  57.6 us (3%)
  other arithmetic  31.7 us (2%)
    reduce_scatter x1, waiting for transfers between devices, local(): lax.psum_scatter(terms[5].astype(jnp.bfloat16), 'batch', scatter_dimensio...  152 us
    reduce_scatter x1, waiting for transfers between devices, local(): lax.psum_scatter(terms[6].astype(jnp.bfloat16), 'batch', scatter_dimensio...  152 us
    all_gather x1, waiting for transfers between devices, local(): lax.all_gather(mlp_in, 'batch', axis=0, tiled=True)  122 us
    reduce_scatter x1, waiting for transfers between devices, local(): lax.psum_scatter(terms[3].astype(jnp.bfloat16), 'batch', scatter_dimensio...  121 us
    psum x1, waiting for transfers between devices, local(): grad_table = lax.psum(grad_table, ('batch', 'seq'))  119 us
    all_gather x1, waiting for transfers between devices, local(): lax.all_gather(mlp_out, 'batch', axis=0, tiled=True)  117 us
    all_gather x1, waiting for transfers between devices, local(): lax.all_gather(qkv_self, 'batch', axis=0, tiled=True)  96.9 us
    psum x1, waiting for transfers between devices, local(): lax.psum(shares[0].astype(jnp.bfloat16), 'seq').astype(jnp.float32)  84.5 us
  transfers between devices with their start and end apart: 23, of which 23 were waited for; matrix products, arithmetic and copies ran while one was open for 8% of the time, Pallas kernels for 0%

commit v1 on v0

--- a/solution.py
+++ b/solution.py
@@ -8,6 +8,19 @@
 epsilon = 1e-06
 group_heads = 4
 highest = lax.Precision.HIGHEST
+
+
+def ring_gather(array, axis, dim):
+    ways = lax.axis_size(axis)
+    up = [(d, (d + 1) % ways) for d in range(ways)]
+    down = [(d, (d - 1) % ways) for d in range(ways)]
+    earlier, later = ([array], [array])
+    for _ in range(ways // 2):
+        earlier.append(lax.ppermute(earlier[-1], axis, up))
+    for _ in range((ways - 1) // 2):
+        later.append(lax.ppermute(later[-1], axis, down))
+    line = jnp.concatenate([*earlier[::-1], *later[1:]], axis=dim)
+    return jnp.roll(line, (lax.axis_index(axis) - ways // 2) * array.shape[dim], axis=dim)
 
 
 def modulated_norm(values, shift, scale):
@@ -133,7 +146,7 @@
         lax.all_gather(out_cross, "batch", axis=0, tiled=True),
         lax.all_gather(qkv_self, "batch", axis=0, tiled=True),
         lax.all_gather(out_self, "batch", axis=0, tiled=True),
-        lax.all_gather(mlp_in, "batch", axis=0, tiled=True),
+        ring_gather(mlp_in, "batch", 0),
         lax.all_gather(mlp_out, "batch", axis=0, tiled=True),
     )
     camera_gate = jax.nn.silu(camera.astype(jnp.float32)).astype(jnp.bfloat16)

time: 1940 us -> 1890 us (0.974)
  waiting for transfers between devices: 1620 us -> 1520 us
    ppermute x0 -> x7, waiting for transfers between devices: none -> 175 us  [the longest x4 175 us: ring_gather(): earlier.append(lax.ppermute(earlier[-1], axis, up))]
    all_gather x1 -> x0, waiting for transfers between devices: 122 us -> none  [local(): lax.all_gather(mlp_in, 'batch', axis=0, tiled=True)]
    all_gather x1, waiting for transfers between devices: 117 us -> 25 us  [local(): lax.all_gather(mlp_out, 'batch', axis=0, tiled=True)]
    reduce_scatter x1, waiting for transfers between devices: 35.5 us -> 4.59 us  [local(): lax.psum_scatter(key_terms.astype(jnp.bfloat16), 'seq', scatter_dimension...]
    reduce_scatter x1, waiting for transfers between devices: 5.37 us -> 35.7 us  [local(): lax.psum_scatter(value_terms.astype(jnp.bfloat16), 'seq', scatter_dimensi...]
    all_gather x1, waiting for transfers between devices: 24.1 us -> 0.01 us  [local(): lax.all_gather(out_self, 'batch', axis=0, tiled=True)]
    unnamed x123 -> x158, local copies, waits for them, and re-layouts: 5.86 us -> 27.4 us
    all_gather x1, waiting for transfers between devices: 20.9 us -> 0.01 us  [local(): lax.all_gather(value_local, 'seq', axis=0, tiled=True)]
  transfers between devices with their start and end apart: 23 -> 29, of which waited for: 23 -> 23; matrix products, arithmetic and copies ran while one was open for 8% -> 9% of each run, Pallas kernels for 0% -> 0%
where the time goes in v1:
time: 1890 us; the launch traced here: 1880 us
  waiting for transfers between devices  1520 us (80%)
  matrix products  206 us (11%)
  local copies, waits for them, and re-layouts  76.9 us (4%)
  other arithmetic  30.1 us (2%)
    ppermute x4, waiting for transfers between devices, ring_gather(): earlier.append(lax.ppermute(earlier[-1], axis, up))  175 us
    reduce_scatter x1, waiting for transfers between devices, local(): lax.psum_scatter(terms[6].astype(jnp.bfloat16), 'batch', scatter_dimensio...  152 us
    reduce_scatter x1, waiting for transfers between devices, local(): lax.psum_scatter(terms[5].astype(jnp.bfloat16), 'batch', scatter_dimensio...  152 us
    reduce_scatter x1, waiting for transfers between devices, local(): lax.psum_scatter(terms[3].astype(jnp.bfloat16), 'batch', scatter_dimensio...  121 us
    psum x1, waiting for transfers between devices, local(): grad_table = lax.psum(grad_table, ('batch', 'seq'))  119 us
    all_gather x1, waiting for transfers between devices, local(): lax.all_gather(qkv_self, 'batch', axis=0, tiled=True)  96.9 us
    psum x1, waiting for transfers between devices, local(): lax.psum(shares[0].astype(jnp.bfloat16), 'seq').astype(jnp.float32)  84.5 us
    reduce_scatter x1, waiting for transfers between devices, local(): lax.psum_scatter(terms[1].astype(jnp.bfloat16), 'batch', scatter_dimensio...  78 us
  transfers between devices with their start and end apart: 29, of which 23 were waited for; matrix products, arithmetic and copies ran while one was open for 9% of the time, Pallas kernels for 0%

profile of v1, /device:TPU:0, one launch (start us, length us, event | category | flops | bytes accessed | tf_op | source)
XLA Modules:
  0.0 1875.6 jit_solution(8187923995961469585)
XLA Ops:
  15.5 69.2 %all-reduce.5.cloned.1.call-done = f32[8,6144]{1,0:T(8,128)} async-done(((f32[8,6144]{1,0:T(8,128)}), f32[8,6144]{1,0:T(8,128)}) %all-reduce.5.cloned.1.call-update) | async-done | bytes 196624 | tf_op jit(solution)/shard_map/psum | solution.py:153
  85.7 49.7 %all-gather.9.cloned.1.call-done = bf16[1024,1024]{1,0:T(8,128)(2,1)} async-done(((bf16[128,1024]{1,0:T(8,128)(2,1)}), bf16[1024,1024]{1,0:T(8,128)(2,1)}) %all-gather.9.cloned.1.call-update) | async-done | bytes 2097168 | tf_op jit(solution)/shard_map/all_gather | solution.py:144
  138.0 58.8 %all-gather.11.cloned.1.call-done = bf16[768,2048]{1,0:T(8,128)(2,1)} async-done(((bf16[96,2048]{1,0:T(8,128)(2,1)}), bf16[768,2048]{1,0:T(8,128)(2,1)}) %all-gather.11.cloned.1.call-update) | async-done | bytes 3145744 | tf_op jit(solution)/shard_map/all_gather | solution.py:145
  196.8 5.6 convolution_convert_fusion.2
  205.0 4.0 copy.35
  209.0 4.0 copy.36
  213.1 18.5 while.56
  231.6 15.3 all-gather.13.cloned.1.call-done
  249.9 96.9 %all-gather.15.cloned.1.call-done = bf16[1024,3072]{1,0:T(8,128)(2,1)} async-done(((bf16[128,3072]{1,0:T(8,128)(2,1)}), bf16[1024,3072]{1,0:T(8,128)(2,1)}) %all-gather.15.cloned.1.call-update) | async-done | bytes 6291472 | tf_op jit(solution)/shard_map/all_gather | solution.py:147
  346.8 4.7 convolution_convert_fusion.4
  354.3 26.7 %collective-permute-done = bf16[128,4096]{1,0:T(8,128)(2,1)} collective-permute-done((bf16[128,4096]{1,0:T(8,128)(2,1)}, bf16[128,4096]{1,0:T(8,128)(2,1)}, u32[]{:S(2)}, u32[]{:S(2)}) %collective-permute-start) | collective-permute-done | bytes 1048608 | tf_op jit(solution)/shard_map/ppermute | solution.py:19
  381.0 4.7 collective-permute-start.4
  385.7 41.5 %collective-permute-done.1 = bf16[128,4096]{1,0:T(8,128)(2,1)S(1)} collective-permute-done((bf16[128,4096]{1,0:T(8,128)(2,1)}, bf16[128,4096]{1,0:T(8,128)(2,1)S(1)}, u32[]{:S(2)}, u32[]{:S(2)}) %collective-permute-start.1) | collective-permute-done | bytes 1048608 | tf_op jit(solution)/shard_map/ppermute | solution.py:19
  432.9 53.2 %collective-permute-done.2 = bf16[128,4096]{1,0:T(8,128)(2,1)} collective-permute-done((bf16[128,4096]{1,0:T(8,128)(2,1)S(1)}, bf16[128,4096]{1,0:T(8,128)(2,1)}, u32[]{:S(2)}, u32[]{:S(2)}) %collective-permute-start.2) | collective-permute-done | bytes 1048608 | tf_op jit(solution)/shard_map/ppermute | solution.py:19
  491.3 53.7 %collective-permute-done.3 = bf16[128,4096]{1,0:T(8,128)(2,1)} collective-permute-done((bf16[128,4096]{1,0:T(8,128)(2,1)}, bf16[128,4096]{1,0:T(8,128)(2,1)}, u32[]{:S(2)}, u32[]{:S(2)}) %collective-permute-start.3) | collective-permute-done | bytes 1048608 | tf_op jit(solution)/shard_map/ppermute | solution.py:19
  558.6 6.6 copy-done.51
  566.5 3.9 copy.38
  570.5 3.9 copy.39
  575.2 22.2 %while.57 = (s32[]{:T(128)}, bf16[4,4,256,64]{2,3,1,0:T(8,128)(2,1)}, f32[4,4,256,1]{2,1,3,0:T(4,128)S(1)}, f32[4,4,256,1]{2,1,3,0:T(4,128)S(1)}, bf16[4,4,256,6...) while((s32[]{:T(128)}, ...), condition=%wide.region_12.13_spmd, body=%wide.region_9.12_spmd.sunk | while | flops 277870592 | bytes 14063705 | solution.py:78
  601.0 7.9 fusion.91
  608.9 25.0 %all-gather.23.cloned.1.call-done = bf16[4096,1024]{1,0:T(8,128)(2,1)} async-done(((bf16[512,1024]{1,0:T(8,128)(2,1)}), bf16[4096,1024]{1,0:T(8,128)(2,1)}) %all-gather.23.cloned.1.call-update) | async-done | bytes 8388624 | tf_op jit(solution)/shard_map/all_gather | solution.py:150
  633.9 9.2 fusion.99
  643.1 7.4 multiply_reduce_fusion.3
  657.4 47.9 %while.58 = (s32[]{:T(128)}, bf16[4,4,256,64]{2,3,1,0:T(8,128)(2,1)}, f32[4,4,1024,64]{2,3,1,0:T(8,128)}, f32[4,4,1024,64]{2,3,1,0:T(8,128)}, bf16[4,4,256,64]{2...) while((s32[]{:T(128)}, ...), condition=%wide.region_19.20_spmd, body=%wide.region_17.19_spmd.sunk | while | flops 680852480 | bytes 44340364 | solution.py:113
  706.2 42.0 %reduce-scatter.12.cloned.1.call-done = f32[256,1024]{0,1:T(8,128)} async-done(((f32[1024,1024]{0,1:T(8,128)}), f32[256,1024]{0,1:T(8,128)}) %reduce-scatter.12.cloned.1.call-update) | async-done | bytes 1048592 | tf_op jit(solution)/shard_map/reduce_scatter | solution.py:207
  749.5 45.8 %reduce-scatter.14.cloned.1.call-done = f32[256,1024]{0,1:T(8,128)} async-done(((f32[1024,1024]{0,1:T(8,128)}), f32[256,1024]{0,1:T(8,128)}) %reduce-scatter.14.cloned.1.call-update) | async-done | bytes 1048592 | tf_op jit(solution)/shard_map/reduce_scatter | solution.py:208
  796.6 5.9 multiply_reduce_fusion.4
  808.6 46.1 %while.59 = (s32[]{:T(128)}, bf16[4,4,256,64]{2,3,1,0:T(8,128)(2,1)}, bf16[4,4,1025,64]{2,3,1,0:T(8,128)(2,1)}, bf16[4,4,1025,64]{2,3,1,0:T(8,128)(2,1)}, pred[1...) while((s32[]{:T(128)}, ...), condition=%wide.region_26.27_spmd, body=%wide.region_24.26_spmd.sunk | while | flops 682566912 | bytes 65885444 | solution.py:113
  855.8 3.1 convolution_convert_fusion.5
  859.2 3.7 convolution_convert_fusion.6
  863.0 3.3 convolution_convert_fusion.7
  866.4 8.6 convolution_convert_fusion
  875.7 7.7 convolution_convert_fusion.1
  883.4 4.6 reduce-scatter.18.cloned.1.call-done
  888.0 35.7 %reduce-scatter.20.cloned.1.call-done = bf16[1025,256]{0,1:T(8,128)(2,1)} async-done(((bf16[1025,1024]{0,1:T(8,128)(2,1)}), bf16[1025,256]{0,1:T(8,128)(2,1)}) %reduce-scatter.20.cloned.1.call-update) | async-done | bytes 524816 | tf_op jit(solution)/shard_map/reduce_scatter | solution.py:225
  933.7 6.2 convolution_convert_fusion.3
  946.3 48.9 %reduce-scatter.28.cloned.1.call-done = bf16[128,1024]{1,0:T(8,128)(2,1)} async-done(((bf16[1024,1024]{1,0:T(8,128)(2,1)}), bf16[128,1024]{1,0:T(8,128)(2,1)}) %reduce-scatter.28.cloned.1.call-update) | async-done | bytes 262160 | tf_op jit(solution)/shard_map/reduce_scatter | solution.py:288
  995.1 71.2 %reduce-scatter.24.cloned.1.call-done = bf16[128,1024]{1,0:T(8,128)(2,1)} async-done(((bf16[1024,1024]{1,0:T(8,128)(2,1)}), bf16[128,1024]{1,0:T(8,128)(2,1)}) %reduce-scatter.24.cloned.1.call-update) | async-done | bytes 262160 | tf_op jit(solution)/shard_map/reduce_scatter | solution.py:282
  1066.3 71.1 %reduce-scatter.16.cloned.1.call-done = bf16[128,1024]{1,0:T(8,128)(2,1)} async-done(((bf16[1024,1024]{1,0:T(8,128)(2,1)}), bf16[128,1024]{1,0:T(8,128)(2,1)}) %reduce-scatter.16.cloned.1.call-update) | async-done | bytes 262160 | tf_op jit(solution)/shard_map/reduce_scatter | solution.py:276
  1137.4 152.0 %reduce-scatter.32.cloned.1.call-done = bf16[512,1024]{1,0:T(8,128)(2,1)} async-done(((bf16[4096,1024]{1,0:T(8,128)(2,1)}), bf16[512,1024]{1,0:T(8,128)(2,1)}) %reduce-scatter.32.cloned.1.call-update) | async-done | bytes 1048592 | tf_op jit(solution)/shard_map/reduce_scatter | solution.py:294
  1289.4 151.5 %reduce-scatter.30.cloned.1.call-done = bf16[128,4096]{1,0:T(8,128)(2,1)} async-done(((bf16[1024,4096]{1,0:T(8,128)(2,1)}), bf16[128,4096]{1,0:T(8,128)(2,1)}) %reduce-scatter.30.cloned.1.call-update) | async-done | bytes 1048592 | tf_op jit(solution)/shard_map/reduce_scatter | solution.py:291
  1441.0 78.0 %reduce-scatter.22.cloned.1.call-done = bf16[96,2048]{1,0:T(8,128)(2,1)} async-done(((bf16[768,2048]{1,0:T(8,128)(2,1)}), bf16[96,2048]{1,0:T(8,128)(2,1)}) %reduce-scatter.22.cloned.1.call-update) | async-done | bytes 393232 | tf_op jit(solution)/shard_map/reduce_scatter | solution.py:279
  1519.0 121.0 %reduce-scatter.26.cloned.1.call-done = bf16[128,3072]{1,0:T(8,128)(2,1)} async-done(((bf16[1024,3072]{1,0:T(8,128)(2,1)}), bf16[128,3072]{1,0:T(8,128)(2,1)}) %reduce-scatter.26.cloned.1.call-update) | async-done | bytes 786448 | tf_op jit(solution)/shard_map/reduce_scatter | solution.py:285
  1640.1 8.3 fusion.112
  1649.8 119.5 %all-reduce.7.cloned.1.call-done = f32[8,6144]{1,0:T(8,128)} async-done(((f32[8,6144]{1,0:T(8,128)}), f32[8,6144]{1,0:T(8,128)}) %all-reduce.7.cloned.1.call-update) | async-done | bytes 196624 | tf_op jit(solution)/shard_map/psum | solution.py:258
  1769.2 4.0 fusion.161
  1773.3 84.5 %all-reduce.9.cloned.1.call-done = (bf16[128,1024]{1,0:T(8,128)(2,1)}, bf16[96,2048]{1,0:T(8,128)(2,1)}, bf16[128,1024]{1,0:T(8,128)(2,1)}, bf16[128,3072]{1,0:T...) async-done(((bf16[128,1024]{1,0:T(8,128)(2,1)}, bf16[96,2048]{1,0:T(8,128)(2,1)}, bf16[128,1024]{1,0:T(8,128)(2,1)}, ...) | async-done | bytes 4063248 | tf_op jit(solution)/shard_map/psum | solution.py:299
  1857.8 2.9 convert_element_type.231
  (418 shorter events, 218.6 us)
Async XLA Ops:
  7.2 189.7 %copy-start = (bf16[1,1025,768]{2,1,0:T(8,128)(2,1)S(1)}, bf16[1,1025,768]{2,1,0:T(8,128)(2,1)}, u32[]{:S(2)}) copy-start(bf16[1,1025,768]{2,1,0:T(8,128)(2,1)} %param.24) | copy-start | bytes 4723204
  7.2 77.5 %all-reduce.5.cloned.1.call-start = ((), (), s32[]{:S(2)}) async-start(), calls=%async_computation.11 | async-start | bytes 393216 | tf_op jit(solution)/shard_map/psum | solution.py:153
  9.8 125.6 %all-gather.9.cloned.1.call-start = ((), (), s32[]{:S(2)}) async-start(), calls=%async_computation.12 | async-start | bytes 2359296 | tf_op jit(solution)/shard_map/all_gather | solution.py:144
  10.6 186.2 %all-gather.11.cloned.1.call-start = ((), (), s32[]{:S(2)}) async-start(), calls=%async_computation.13 | async-start | bytes 3538944 | tf_op jit(solution)/shard_map/all_gather | solution.py:145
  11.3 235.6 %all-gather.13.cloned.1.call-start = ((), (), s32[]{:S(2)}) async-start(), calls=%async_computation.14 | async-start | bytes 2359296 | tf_op jit(solution)/shard_map/all_gather | solution.py:146
  11.9 334.9 %all-gather.15.cloned.1.call-start = ((), (), s32[]{:S(2)}) async-start(), calls=%async_computation.15 | async-start | bytes 7077888 | tf_op jit(solution)/shard_map/all_gather | solution.py:147
  12.5 554.0 %all-gather.17.cloned.1.call-start = ((), (), s32[]{:S(2)}) async-start(), calls=%async_computation.16 | async-start | bytes 2621440 | tf_op jit(solution)/shard_map/all_gather | solution.py:180
  15.1 187.3 %copy-start.52 = (f32[256]{0:T(256)}, f32[256]{0:T(256)S(1)}, u32[]{:S(2)}) copy-start(f32[256]{0:T(256)S(1)} %broadcast_multiply_fusion.2) | copy-start | bytes 3076
  15.4 120.0 %copy-start.66 = (f32[256]{0:T(256)}, f32[256]{0:T(256)S(1)}, u32[]{:S(2)}) copy-start(f32[256]{0:T(256)S(1)} %fusion.121) | copy-start | bytes 3076
  15.4 187.0 %copy-start.58 = (f32[256]{0:T(256)}, f32[256]{0:T(256)S(1)}, u32[]{:S(2)}) copy-start(f32[256]{0:T(256)S(1)} %fusion.155) | copy-start | bytes 3076
  85.7 116.8 %copy-start.48 = (f32[1,1024]{1,0:T(1,128)}, f32[1,1024]{1,0:T(1,128)S(1)}, u32[]{:S(2)}) copy-start(f32[1,1024]{1,0:T(1,128)S(1)} %get-tuple-element.337) | copy-start | bytes 12292
  85.7 116.8 %copy-start.64 = (f32[1,1024]{1,0:T(1,128)}, f32[1,1024]{1,0:T(1,128)S(1)}, u32[]{:S(2)}) copy-start(f32[1,1024]{1,0:T(1,128)S(1)} %get-tuple-element.336) | copy-start | bytes 12292
  85.7 261.1 %copy-start.41 = (f32[1,1024]{1,0:T(1,128)}, f32[1,1024]{1,0:T(1,128)S(1)}, u32[]{:S(2)}) copy-start(f32[1,1024]{1,0:T(1,128)S(1)} %get-tuple-element.334) | copy-start | bytes 12292
  85.7 514.6 %copy-start.42 = (f32[1,1024]{1,0:T(1,128)}, f32[1,1024]{1,0:T(1,128)S(1)}, u32[]{:S(2)}) copy-start(f32[1,1024]{1,0:T(1,128)S(1)} %get-tuple-element.338) | copy-start | bytes 12292
  85.7 564.9 %copy-start.39 = (f32[1,1024]{1,0:T(1,128)}, f32[1,1024]{1,0:T(1,128)S(1)}, u32[]{:S(2)}) copy-start(f32[1,1024]{1,0:T(1,128)S(1)} %get-tuple-element.333) | copy-start | bytes 12292
  231.6 119.9 %copy-start.44 = (f32[4,4,256,1]{2,1,3,0:T(4,128)}, f32[4,4,256,1]{2,1,3,0:T(4,128)S(1)}, u32[]{:S(2)}) copy-start(f32[4,4,256,1]{2,1,3,0:T(4,128)S(1)} %get-tuple-element.690) | copy-start | bytes 49156
  231.6 119.9 %copy-start.45 = (f32[4,4,256,1]{2,1,3,0:T(4,128)}, f32[4,4,256,1]{2,1,3,0:T(4,128)S(1)}, u32[]{:S(2)}) copy-start(f32[4,4,256,1]{2,1,3,0:T(4,128)S(1)} %get-tuple-element.691) | copy-start | bytes 49156
  231.6 119.9 %copy-start.46 = (pred[1025]{0:T(1024)(128)(4,1)}, pred[1025]{0:T(1024)(128)(4,1)S(1)}, u32[]{:S(2)}) copy-start(pred[1025]{0:T(1024)(128)(4,1)S(1)} %get-tuple-element.833) | copy-start | bytes 3079
  249.6 552.9 %copy-start.55 = (f32[256]{0:T(256)}, f32[256]{0:T(256)S(1)}, u32[]{:S(2)}) copy-start(f32[256]{0:T(256)S(1)} %broadcast_multiply_fusion.1) | copy-start | bytes 3076
  249.8 101.7 %copy-start.68 = (f32[256]{0:T(256)}, f32[256]{0:T(256)S(1)}, u32[]{:S(2)}) copy-start(f32[256]{0:T(256)S(1)} %multiply_reduce_fusion.8) | copy-start | bytes 3076
  249.9 552.6 %copy-start.61 = (f32[256]{0:T(256)}, f32[256]{0:T(256)S(1)}, u32[]{:S(2)}) copy-start(f32[256]{0:T(256)S(1)} %fusion.156) | copy-start | bytes 3076
  352.7 217.7 %all-gather.19.cloned.1.call-start = ((), (), s32[]{:S(2)}) async-start(), calls=%async_computation.17 | async-start | bytes 2621440 | tf_op jit(solution)/shard_map/all_gather | solution.py:181
  353.5 243.9 %all-gather.21.cloned.1.call-start = ((), (), s32[]{:S(2)}) async-start(), calls=%async_computation.18 | async-start | bytes 2359296 | tf_op jit(solution)/shard_map/all_gather | solution.py:148
  353.5 27.5 %collective-permute-start = (bf16[128,4096]{1,0:T(8,128)(2,1)}, bf16[128,4096]{1,0:T(8,128)(2,1)}, u32[]{:S(2)}, u32[]{:S(2)}) collective-permute-start(bf16[128,4096]{1,0:T(8,128)(2,1)} %param.34), channel_id=1, source_target_pairs={{0,4},{4,8},{8,12},{12,16},{16,20},{20,24},{24,28},{28,0},{1,5},{5... | collective-permute-start | bytes 3145736 | tf_op jit(solution)/shard_map/ppermute | solution.py:19
  354.2 279.7 %all-gather.23.cloned.1.call-start = ((), (), s32[]{:S(2)}) async-start(), calls=%async_computation.19 | async-start | bytes 9437184 | tf_op jit(solution)/shard_map/all_gather | solution.py:150
  381.0 46.2 %collective-permute-start.1 = (bf16[128,4096]{1,0:T(8,128)(2,1)}, bf16[128,4096]{1,0:T(8,128)(2,1)S(1)}, u32[]{:S(2)}, u32[]{:S(2)}) collective-permute-start(bf16[128,4096]{1,0:T(8,128)(2,1)} %collective-permute-done), channel_id=1, source_target_pairs={{0,4},{4,8},{8,12},{12,16},{16,20},{20,24},{24,28},{28,0},{1,5},{5... | collective-permute-start | bytes 3145736 | tf_op jit(solution)/shard_map/ppermute | solution.py:19
  381.0 49.6 %collective-permute-start.4 = (bf16[128,4096]{1,0:T(8,128)(2,1)}, bf16[128,4096]{1,0:T(8,128)(2,1)}, u32[]{:S(2)}, u32[]{:S(2)}) collective-permute-start(bf16[128,4096]{1,0:T(8,128)(2,1)} %param.34), channel_id=1, source_target_pairs={{0,28},{4,0},{8,4},{12,8},{16,12},{20,16},{24,20},{28,24},{1,29},{... | collective-permute-start | bytes 3145736 | tf_op jit(solution)/shard_map/ppermute | solution.py:21
  428.2 58.0 %collective-permute-start.2 = (bf16[128,4096]{1,0:T(8,128)(2,1)S(1)}, bf16[128,4096]{1,0:T(8,128)(2,1)}, u32[]{:S(2)}, u32[]{:S(2)}) collective-permute-start(bf16[128,4096]{1,0:T(8,128)(2,1)S(1)} %collective-permute-done.1), channel_id=1, source_target_pairs={{0,4},{4,8},{8,12},{12,16},{16,20},{20,24},{24,28},{28,0},{1,5},{5... | collective-permute-start | bytes 3145736 | tf_op jit(solution)/shard_map/ppermute | solution.py:19
  430.6 58.3 %collective-permute-start.5 = (bf16[128,4096]{1,0:T(8,128)(2,1)}, bf16[128,4096]{1,0:T(8,128)(2,1)}, u32[]{:S(2)}, u32[]{:S(2)}) collective-permute-start(bf16[128,4096]{1,0:T(8,128)(2,1)} %collective-permute-done.4), channel_id=1, source_target_pairs={{0,28},{4,0},{8,4},{12,8},{16,12},{20,16},{24,20},{28,24},{1,29},{... | collective-permute-start | bytes 3145736 | tf_op jit(solution)/shard_map/ppermute | solution.py:21
  486.1 58.9 %collective-permute-start.3 = (bf16[128,4096]{1,0:T(8,128)(2,1)}, bf16[128,4096]{1,0:T(8,128)(2,1)}, u32[]{:S(2)}, u32[]{:S(2)}) collective-permute-start(bf16[128,4096]{1,0:T(8,128)(2,1)} %collective-permute-done.2), channel_id=1, source_target_pairs={{0,4},{4,8},{8,12},{12,16},{16,20},{20,24},{24,28},{28,0},{1,5},{5... | collective-permute-start | bytes 3145736 | tf_op jit(solution)/shard_map/ppermute | solution.py:19
  488.7 259.5 %reduce-scatter.12.cloned.1.call-start = ((), (), s32[]{:S(2)}) async-start(), calls=%async_computation.20 | async-start | bytes 5242880 | tf_op jit(solution)/shard_map/reduce_scatter | solution.py:207
  488.8 58.8 %copy-start.20 = (bf16[128,4096]{1,0:T(8,128)(2,1)S(1)}, bf16[128,4096]{1,0:T(8,128)(2,1)}, u32[]{:S(2)}) copy-start(bf16[128,4096]{1,0:T(8,128)(2,1)} %copy-done.19) | copy-start | bytes 3145732
  488.8 60.2 %copy-start.18 = (bf16[128,4096]{1,0:T(8,128)(2,1)S(1)}, bf16[128,4096]{1,0:T(8,128)(2,1)}, u32[]{:S(2)}) copy-start(bf16[128,4096]{1,0:T(8,128)(2,1)} %param.34) | copy-start | bytes 3145732
  488.9 62.9 %collective-permute-start.6 = (bf16[128,4096]{1,0:T(8,128)(2,1)}, bf16[128,4096]{1,0:T(8,128)(2,1)S(1)}, u32[]{:S(2)}, u32[]{:S(2)}) collective-permute-start(bf16[128,4096]{1,0:T(8,128)(2,1)} %collective-permute-done.5), channel_id=1, source_target_pairs={{0,28},{4,0},{8,4},{12,8},{16,12},{20,16},{24,20},{28,24},{1,29},{... | collective-permute-start | bytes 3145736 | tf_op jit(solution)/shard_map/ppermute | solution.py:21
  705.4 89.9 %reduce-scatter.14.cloned.1.call-start = ((), (), s32[]{:S(2)}) async-start(), calls=%async_computation.21 | async-start | bytes 5242880 | tf_op jit(solution)/shard_map/reduce_scatter | solution.py:208
  706.1 181.9 %reduce-scatter.18.cloned.1.call-start = ((), (), s32[]{:S(2)}) async-start(), calls=%async_computation.24 | async-start | bytes 2949120 | tf_op jit(solution)/shard_map/reduce_scatter | solution.py:222
  854.8 68.9 %reduce-scatter.20.cloned.1.call-start = ((), (), s32[]{:S(2)}) async-start(), calls=%async_computation.25 | async-start | bytes 2949120 | tf_op jit(solution)/shard_map/reduce_scatter | solution.py:225
  855.6 139.6 %reduce-scatter.28.cloned.1.call-start = ((), (), s32[]{:S(2)}) async-start(), calls=%async_computation.29 | async-start | bytes 2359296 | tf_op jit(solution)/shard_map/reduce_scatter | solution.py:288
  858.9 207.4 %reduce-scatter.24.cloned.1.call-start = ((), (), s32[]{:S(2)}) async-start(), calls=%async_computation.27 | async-start | bytes 2359296 | tf_op jit(solution)/shard_map/reduce_scatter | solution.py:282
  862.9 274.5 %reduce-scatter.16.cloned.1.call-start = ((), (), s32[]{:S(2)}) async-start(), calls=%async_computation.23 | async-start | bytes 2359296 | tf_op jit(solution)/shard_map/reduce_scatter | solution.py:276
  866.3 423.1 %reduce-scatter.32.cloned.1.call-start = ((), (), s32[]{:S(2)}) async-start(), calls=%async_computation.31 | async-start | bytes 9437184 | tf_op jit(solution)/shard_map/reduce_scatter | solution.py:294
  875.0 566.0 %reduce-scatter.30.cloned.1.call-start = ((), (), s32[]{:S(2)}) async-start(), calls=%async_computation.30 | async-start | bytes 9437184 | tf_op jit(solution)/shard_map/reduce_scatter | solution.py:291
  883.4 635.6 %reduce-scatter.22.cloned.1.call-start = ((), (), s32[]{:S(2)}) async-start(), calls=%async_computation.26 | async-start | bytes 3538944 | tf_op jit(solution)/shard_map/reduce_scatter | solution.py:279
  933.6 706.4 %reduce-scatter.26.cloned.1.call-start = ((), (), s32[]{:S(2)}) async-start(), calls=%async_computation.28 | async-start | bytes 7077888 | tf_op jit(solution)/shard_map/reduce_scatter | solution.py:285
  939.9 700.1 %copy-start.5 = (f32[256,1024]{1,0:T(8,128)S(1)}, f32[256,1024]{1,0:T(8,128)}, u32[]{:S(2)}) copy-start(f32[256,1024]{1,0:T(8,128)} %copy-done.3) | copy-start | bytes 3145732
  939.9 829.3 %all-reduce.7.cloned.1.call-start = ((), (), s32[]{:S(2)}) async-start(), calls=%async_computation.22 | async-start | bytes 393216 | tf_op jit(solution)/shard_map/psum | solution.py:258
  946.2 911.6 %all-reduce.9.cloned.1.call-start = ((), (), s32[]{:S(2)}) async-start(), calls=%async_computation.32 | async-start | bytes 8126464 | tf_op jit(solution)/shard_map/psum | solution.py:299
  1640.0 129.2 %copy-start.70 = (bf16[8,128]{1,0:T(8,128)(2,1)S(1)}, bf16[8,128]{1,0:T(8,128)(2,1)}, u32[]{:S(2)}) copy-start(bf16[8,128]{1,0:T(8,128)(2,1)} %param.27) | copy-start | bytes 6148
  (74 other events, 418.9 us)
Sparse Core Ops, SparseCore 0:
  11.9 72.7 all-reduce.4
  87.1 48.3 all-gather.8
  137.9 58.9 all-gather.10
  199.0 47.8 all-gather.12
  249.2 97.5 all-gather.14
  352.8 20.7 all-gather.16
  375.9 22.5 all-gather.18
  400.8 81.8 all-gather.20
  488.9 144.9 all-gather.22
  705.5 42.6 reduce-scatter.11
  750.7 44.4 reduce-scatter.13
  854.9 33.0 reduce-scatter.17
  890.6 33.0 reduce-scatter.19
  927.5 67.5 reduce-scatter.27
  999.5 66.8 reduce-scatter.23
  1070.7 66.6 reduce-scatter.15
  1141.3 148.0 reduce-scatter.31
  1292.9 148.0 reduce-scatter.29
  1445.5 73.4 reduce-scatter.21
  1522.8 117.0 reduce-scatter.25
  1647.0 122.1 all-reduce.6
  1772.3 85.3 all-reduce.8
